TPU v7x, 32 devices: a whole 2x2x4 slice. The times are simulated.
32 devices in a mesh: rot: 8 (over y, x, core), az: 4 (over z).
Axes of the slice: x: 2, y: 2, z: 4, core: 2. Of those that a mesh axis runs over, the one named last changes fastest.
Arguments:
- inputs: bfloat16 [16, 4, 128, 128], P('rot', None, 'az'), may hold values from -6 to 6
- pre_one: bfloat16 [16, 4, 128, 128], P('rot', None, 'az'), may hold values from -8 to 8
- pre_two: bfloat16 [16, 4, 128, 128], P('rot', None, 'az'), may hold values from -8 to 8
- cotangent: bfloat16 [16, 4, 128, 128], P('rot', None, 'az'), may hold values from -6 to 6
- filt_one: bfloat16 [16, 3, 3, 128, 128], P('rot'), may hold values from -0.046875 to 0.046875
- filt_two: bfloat16 [16, 3, 3, 128, 128], P('rot'), may hold values from -0.046875 to 0.046875
Outputs:
- input_grad: bfloat16 [16, 4, 128, 128], P('rot', None, 'az')
- filt_grad_one: float32 [16, 3, 3, 128, 128], P('rot')
- filt_grad_two: float32 [16, 3, 3, 128, 128], P('rot')
All inputs are finite; a program needn't handle non-finite values.
Results may differ from a plain program's by a relative error of at most 0.018.
Values may be sent and summed in bfloat16 or wider, within the bound.
A program may use at most 64 MiB of HBM per device.

v0:
```python
import jax
import jax.numpy as jnp
from jax import lax
from jax.sharding import PartitionSpec as P


def with_halo(block, sides, width):
    for axis, dim in sides:
        count = lax.axis_size(axis)
        forward = [(i, i + 1) for i in range(count - 1)]
        forward.append((count - 1, 0))
        backward = [(target, source) for source, target in forward]
        low = lax.ppermute(
            lax.slice_in_dim(block, block.shape[dim] - width, None, axis=dim), axis, forward
        )
        high = lax.ppermute(lax.slice_in_dim(block, 0, width, axis=dim), axis, backward)
        block = jnp.concatenate([low, block, high], axis=dim)
    return block


def slope(pre):
    widened = pre.astype(jnp.float32)
    logistic = jax.nn.sigmoid(widened)
    return logistic * (1.0 + widened * (1.0 - logistic))


def pad_rows(field):
    return jnp.pad(field, ((0, 0), (1, 1), (0, 0), (0, 0)))


def doubled_rows(field):
    padded = pad_rows(field)
    return jnp.concatenate([padded, padded], axis=0)


def filter_terms(features, gradient, my_rank, per_dev):
    doubled = doubled_rows(features)
    orient_count = gradient.shape[0]
    row_count = gradient.shape[1]
    col_count = gradient.shape[2]
    channels = gradient.shape[3]
    results = []
    for slot_index in range(per_dev):
        shifted = lax.dynamic_slice_in_dim(doubled, my_rank * per_dev + slot_index, orient_count, 0)
        pieces = []
        for row_tap in range(3):
            for col_tap in range(3):
                window = shifted[:, row_tap : row_tap + row_count, col_tap : col_tap + col_count, :]
                pieces.append(
                    lax.dot_general(
                        window,
                        gradient,
                        (((0, 1, 2), (0, 1, 2)), ((), ())),
                        preferred_element_type=jnp.float32,
                    )
                )
        results.append(jnp.stack(pieces).reshape(3, 3, channels, channels))
    return jnp.stack(results)


def make_terms(doubled, my_rank, filt_local, row_count, col_count, first_row, row_span):
    orient_count = doubled.shape[0] // 2
    channels = doubled.shape[3]
    per_dev = filt_local.shape[0]
    summed = jnp.zeros((row_span, row_count, col_count, channels), jnp.float32)
    for slot_index in range(per_dev):
        relative = my_rank * per_dev + slot_index
        offset = (first_row - relative) % orient_count
        chosen = lax.dynamic_slice_in_dim(doubled, offset, row_span, 0)
        for row_tap in range(3):
            for col_tap in range(3):
                window = chosen[
                    :,
                    2 - row_tap : 2 - row_tap + row_count,
                    2 - col_tap : 2 - col_tap + col_count,
                    :,
                ]
                summed = summed + lax.dot_general(
                    window,
                    filt_local[slot_index, row_tap, col_tap],
                    (((3,), (1,)), ((), ())),
                    preferred_element_type=jnp.float32,
                )
    return summed


def shards(inputs, pre_one, pre_two, cotangent, filt_one, filt_two):
    per_dev = inputs.shape[0]
    row_count = inputs.shape[1]
    col_count = inputs.shape[2]
    my_rank = lax.axis_index("rot")
    cell_count = per_dev * lax.axis_size("rot") * row_count * col_count * lax.axis_size("az")
    norm_scale = cell_count ** (-0.5)
    act_one = jax.nn.silu(pre_one.astype(jnp.float32)).astype(jnp.bfloat16)
    grad_two = (cotangent.astype(jnp.float32) * slope(pre_two)).astype(jnp.bfloat16)
    stacked = jnp.concatenate([inputs, act_one, grad_two], axis=0)
    widened = with_halo(stacked, (("az", 2),), 1)
    inputs_rim = widened[0:per_dev]
    act_rim = widened[per_dev : 2 * per_dev]
    grad_rim = widened[2 * per_dev : 3 * per_dev]
    all_inputs, all_act, all_grad = (
        lax.all_gather(inputs_rim, "rot", axis=0, tiled=True),
        lax.all_gather(act_rim, "rot", axis=0, tiled=True),
        lax.all_gather(grad_rim, "rot", axis=0, tiled=True),
    )
    out_cols = all_grad.shape[2] - 2
    margin = (all_grad.shape[2] - col_count) // 2
    doubled_two = doubled_rows(all_grad)
    delta_one = lax.psum_scatter(
        make_terms(
            doubled_two,
            my_rank,
            filt_two,
            row_count,
            out_cols,
            jnp.int32(0),
            per_dev * lax.axis_size("rot"),
        ),
        "rot",
        scatter_dimension=0,
        tiled=True,
    )
    grad_inner = all_grad[:, :, margin : margin + col_count]
    filt_part_two = filter_terms(all_act, grad_inner, my_rank, per_dev)
    grad_one = (delta_one * slope(pre_one)).astype(jnp.bfloat16)
    grad_one_rim = with_halo(grad_one, (("az", 2),), 1)
    all_grad_one = lax.all_gather(grad_one_rim, "rot", axis=0, tiled=True)
    doubled_one = doubled_rows(all_grad_one)
    input_sum = lax.psum_scatter(
        make_terms(
            doubled_one,
            my_rank,
            filt_one,
            row_count,
            col_count,
            jnp.int32(0),
            lax.axis_size("rot") * per_dev,
        ).astype(jnp.bfloat16),
        "rot",
        scatter_dimension=0,
        tiled=True,
    )
    filt_part_one = filter_terms(all_inputs, all_grad_one[:, :, 1:-1], my_rank, per_dev)
    summed_one, summed_two = (
        lax.psum(filt_part_one.astype(jnp.bfloat16), "az").astype(jnp.float32),
        lax.psum(filt_part_two.astype(jnp.bfloat16), "az").astype(jnp.float32),
    )
    return (input_sum, summed_one * norm_scale, summed_two * norm_scale)


def solution(mesh):
    return jax.shard_map(
        shards,
        mesh=mesh,
        in_specs=(
            P("rot", None, "az", None),
            P("rot", None, "az", None),
            P("rot", None, "az", None),
            P("rot", None, "az", None),
            P("rot", None, None, None, None),
            P("rot", None, None, None, None),
        ),
        out_specs=(
            P("rot", None, "az", None),
            P("rot", None, None, None, None),
            P("rot", None, None, None, None),
        ),
        check_vma=False,
    )
```

profile of v0, /device:TPU:0, one launch (start us, length us, event | category | flops | bytes accessed | tf_op | source)
XLA Modules:
  0.0 203.7 jit_solution(10225011640854622660)
XLA Ops:
  7.2 1.0 fusion.197
  9.0 5.1 %collective-permute-start.1 = (bf16[6,4,1,128]{3,2,1,0:T(2,128)(2,1)S(1)}, bf16[6,4,1,128]{3,2,1,0:T(2,128)(2,1)S(1)}, u32[]{:S(2)}, u32[]{:S(2)}) collective-permute-start(bf16[6,4,1,128]{3,2,1,0:T(2,128)(2,1)S(1)} %get-tuple-element.17), channel_id=1, source_target_pairs={{1,0},{2,1},{3,2},{0,3},{5,4},{6,5},{7,6},{4,7},{9,8},{10,9},{11,1... | collective-permute-start | bytes 18440 | tf_op jit(solution)/shard_map/ppermute | solution.py:16
  14.1 1.4 collective-permute-done.1
  15.5 4.1 %collective-permute-done = bf16[6,4,1,128]{3,2,1,0:T(2,128)(2,1)S(1)} collective-permute-done((bf16[6,4,1,128]{3,2,1,0:T(2,128)(2,1)S(1)}, bf16[6,4,1,128]{3,2,1,0:T(2,128)(2,1)S(1)}, u32[]{:S(2)}, u32[]{:S(2)}) %collective-permute-start) | collective-permute-done | bytes 6176 | tf_op jit(solution)/shard_map/ppermute | solution.py:13
  19.6 1.0 pad_maximum_fusion.2
  20.6 10.0 %all_gather.12 = bf16[16,4,34,128]{3,1,2,0:T(4,128)(2,1)S(1)} all-gather(bf16[2,4,34,128]{3,1,2,0:T(4,128)(2,1)S(1)} %copy.9), channel_id=1, replica_groups=mesh['rot'=8,'az'=4] {'rot'}, dimensions={0}, use_global_device_ids=true | all-gather | bytes 626688 | tf_op jit(solution)/shard_map/all_gather | solution.py:104
  37.3 1.3 convolution_add_fusion.17
  38.7 10.0 %all_gather.14 = bf16[16,4,34,128]{3,1,2,0:T(4,128)(2,1)S(1)} all-gather(bf16[2,4,34,128]{3,1,2,0:T(4,128)(2,1)S(1)} %copy.13), channel_id=1, replica_groups=mesh['rot'=8,'az'=4] {'rot'}, dimensions={0}, use_global_device_ids=true | all-gather | bytes 626688 | tf_op jit(solution)/shard_map/all_gather | solution.py:102
  48.9 9.2 %all_gather.15 = bf16[16,4,34,128]{3,1,2,0:T(4,128)(2,1)S(1)} all-gather(bf16[2,4,34,128]{3,1,2,0:T(4,128)(2,1)S(1)} %copy.16), channel_id=1, replica_groups=mesh['rot'=8,'az'=4] {'rot'}, dimensions={0}, use_global_device_ids=true | all-gather | bytes 626688 | tf_op jit(solution)/shard_map/all_gather | solution.py:103
  64.0 1.7 fusion.112
  68.1 3.8 %reduce-scatter.3.cloned.1.call-done = f32[2,4,32,128]{3,2,1,0:T(8,128)} async-done(((f32[16,4,32,128]{3,2,1,0:T(8,128)}), f32[2,4,32,128]{3,2,1,0:T(8,128)}) %reduce-scatter.3.cloned.1.call-update) | async-done | bytes 131088 | tf_op jit(solution)/shard_map/reduce_scatter | solution.py:109
  72.0 1.0 fusion.205
  73.0 3.4 %collective-permute-start.3 = (bf16[2,4,1,128]{3,2,1,0:T(2,128)(2,1)S(1)}, bf16[2,4,1,128]{3,2,1,0:T(2,128)(2,1)S(1)}, u32[]{:S(2)}, u32[]{:S(2)}) collective-permute-start(bf16[2,4,1,128]{3,2,1,0:T(2,128)(2,1)S(1)} %get-tuple-element.19), channel_id=1, source_target_pairs={{1,0},{2,1},{3,2},{0,3},{5,4},{6,5},{7,6},{4,7},{9,8},{10,9},{11,1... | collective-permute-start | bytes 6152 | tf_op jit(solution)/shard_map/ppermute | solution.py:16
  77.7 4.1 %collective-permute-done.2 = bf16[2,4,1,128]{3,2,1,0:T(2,128)(2,1)S(1)} collective-permute-done((bf16[2,4,1,128]{3,2,1,0:T(2,128)(2,1)S(1)}, bf16[2,4,1,128]{3,2,1,0:T(2,128)(2,1)S(1)}, u32[]{:S(2)}, u32[]{:S(2)}) %collective-permute-start.2) | collective-permute-done | bytes 2080 | tf_op jit(solution)/shard_map/ppermute | solution.py:13
  81.8 10.2 %all_gather.13 = bf16[16,4,34,128]{3,1,2,0:T(4,128)(2,1)S(1)} all-gather(bf16[2,4,34,128]{3,1,2,0:T(4,128)(2,1)S(1)} %copy.11), channel_id=1, replica_groups=mesh['rot'=8,'az'=4] {'rot'}, dimensions={0}, use_global_device_ids=true | all-gather | bytes 626688 | tf_op jit(solution)/shard_map/all_gather | solution.py:127
  106.6 1.1 convolution_add_fusion.4
  107.7 1.1 convolution_add_fusion.3
  108.7 1.1 convolution_add_fusion.2
  109.8 1.1 convolution_add_fusion.1
  110.9 1.9 fusion
  112.8 47.2 %all-reduce.7.cloned.1.call-done = (bf16[2,3,3,128,128]{4,3,2,1,0:T(8,128)(2,1)}, bf16[2,3,3,128,128]{4,3,2,1,0:T(8,128)(2,1)}) async-done(((bf16[2,3,3,128,128]{4,3,2,1,0:T(8,128)(2,1)}, bf16[2,3,3,128,128]{4,3,2,1,0:T(8,128)(2,1)}), (bf16[2,3,3,128,128]{4,3,2,1,0:T(8,128)(2,1)}, bf16[2,3,3,128,128]{4,3,2,1,0:T(8,128)(2,1)})) %all-reduce.7.cloned.1.call-update) | async-done | bytes 1179664 | tf_op jit(solution)/shard_map/psum | solution.py:145
  159.9 2.3 %convert_multiply_fusion.1 = f32[2,3,3,128,128]{4,3,2,1,0:T(8,128)} fusion(bf16[2,3,3,128,128]{4,3,2,1,0:T(8,128)(2,1)} %get-tuple-element.3), kind=kLoop, calls=%fused_computation.52 | loop fusion | flops 589824 | bytes 1769472 | tf_op jit(solution)/shard_map/mul | solution.py:148
  162.2 1.2 convert_multiply_fusion
  163.4 33.8 %reduce-scatter.5.cloned.1.call-done = bf16[2,4,32,128]{3,2,1,0:T(8,128)(2,1)} async-done(((bf16[16,4,32,128]{3,2,1,0:T(8,128)(2,1)}), bf16[2,4,32,128]{3,2,1,0:T(8,128)(2,1)}) %reduce-scatter.5.cloned.1.call-update) | async-done | bytes 65552 | tf_op jit(solution)/shard_map/reduce_scatter | solution.py:129
  (106 shorter events, 31.9 us)
Async XLA Ops:
  7.2 64.8 %reduce-scatter.3.cloned.1.call-start = ((), (), s32[]{:S(2)}) async-start(), calls=%async_computation.2 | async-start | bytes 1179648 | tf_op jit(solution)/shard_map/reduce_scatter | solution.py:109
  9.0 6.5 %collective-permute-start.1 = (bf16[6,4,1,128]{3,2,1,0:T(2,128)(2,1)S(1)}, bf16[6,4,1,128]{3,2,1,0:T(2,128)(2,1)S(1)}, u32[]{:S(2)}, u32[]{:S(2)}) collective-permute-start(bf16[6,4,1,128]{3,2,1,0:T(2,128)(2,1)S(1)} %get-tuple-element.17), channel_id=1, source_target_pairs={{1,0},{2,1},{3,2},{0,3},{5,4},{6,5},{7,6},{4,7},{9,8},{10,9},{11,1... | collective-permute-start | bytes 18440 | tf_op jit(solution)/shard_map/ppermute | solution.py:16
  14.1 5.5 %collective-permute-start = (bf16[6,4,1,128]{3,2,1,0:T(2,128)(2,1)S(1)}, bf16[6,4,1,128]{3,2,1,0:T(2,128)(2,1)S(1)}, u32[]{:S(2)}, u32[]{:S(2)}) collective-permute-start(bf16[6,4,1,128]{3,2,1,0:T(2,128)(2,1)S(1)} %get-tuple-element.16), channel_id=1, source_target_pairs={{0,1},{1,2},{2,3},{3,0},{4,5},{5,6},{6,7},{7,4},{8,9},{9,10},{10,1... | collective-permute-start | bytes 18440 | tf_op jit(solution)/shard_map/ppermute | solution.py:13
  30.8 1.1 copy-start.3
  38.6 121.4 %all-reduce.7.cloned.1.call-start = ((), (), s32[]{:S(2)}) async-start(), calls=%async_computation.4 | async-start | bytes 2359296 | tf_op jit(solution)/shard_map/psum | solution.py:145
  67.7 4.3 %copy-start.4 = (bf16[2,4,32,128]{3,2,1,0:T(8,128)(2,1)S(1)}, bf16[2,4,32,128]{3,2,1,0:T(8,128)(2,1)}, u32[]{:S(2)}) copy-start(bf16[2,4,32,128]{3,2,1,0:T(8,128)(2,1)} %param.7) | copy-start | bytes 196612
  73.0 4.7 %collective-permute-start.3 = (bf16[2,4,1,128]{3,2,1,0:T(2,128)(2,1)S(1)}, bf16[2,4,1,128]{3,2,1,0:T(2,128)(2,1)S(1)}, u32[]{:S(2)}, u32[]{:S(2)}) collective-permute-start(bf16[2,4,1,128]{3,2,1,0:T(2,128)(2,1)S(1)} %get-tuple-element.19), channel_id=1, source_target_pairs={{1,0},{2,1},{3,2},{0,3},{5,4},{6,5},{7,6},{4,7},{9,8},{10,9},{11,1... | collective-permute-start | bytes 6152 | tf_op jit(solution)/shard_map/ppermute | solution.py:16
  76.3 5.4 %collective-permute-start.2 = (bf16[2,4,1,128]{3,2,1,0:T(2,128)(2,1)S(1)}, bf16[2,4,1,128]{3,2,1,0:T(2,128)(2,1)S(1)}, u32[]{:S(2)}, u32[]{:S(2)}) collective-permute-start(bf16[2,4,1,128]{3,2,1,0:T(2,128)(2,1)S(1)} %get-tuple-element.18), channel_id=1, source_target_pairs={{0,1},{1,2},{2,3},{3,0},{4,5},{5,6},{6,7},{7,4},{8,9},{9,10},{10,1... | collective-permute-start | bytes 6152 | tf_op jit(solution)/shard_map/ppermute | solution.py:13
  92.2 1.1 copy-start.2
  97.0 1.2 copy-start
  106.5 90.6 %reduce-scatter.5.cloned.1.call-start = ((), (), s32[]{:S(2)}) async-start(), calls=%async_computation.3 | async-start | bytes 589824 | tf_op jit(solution)/shard_map/reduce_scatter | solution.py:129
  159.9 2.3 %copy-start.1 = (bf16[2,3,3,128,128]{4,3,2,1,0:T(8,128)(2,1)S(1)}, bf16[2,3,3,128,128]{4,3,2,1,0:T(8,128)(2,1)}, u32[]{:S(2)}) copy-start(bf16[2,3,3,128,128]{4,3,2,1,0:T(8,128)(2,1)} %get-tuple-element.4) | copy-start | bytes 1769476
Sparse Core Ops, SparseCore 0:
  38.7 33.2 reduce-scatter.2
  106.6 53.2 all-reduce.6
  163.6 33.5 reduce-scatter.4
where the time goes:
time: 205 us; the launch traced here: 204 us
  waiting for transfers between devices  94.8 us (46%)
  blocking collectives  39.3 us (19%)
  matrix products  31.5 us (15%)
  between operations  14.1 us (7%)
  other arithmetic  13 us (6%)
  starting transfers between devices  8.63 us (4%)
  local copies, waits for them, and re-layouts  2.34 us (1%)
    psum x1, waiting for transfers between devices, shards(): lax.psum(filt_part_one.astype(jnp.bfloat16), 'az').astype(jnp.float32)  47.2 us
    reduce_scatter x1, waiting for transfers between devices, shards(): lax.psum_scatter(make_terms(doubled_one, my_rank, filt_one, row_count, co...  33.8 us
    dot_general x36, matrix products, make_terms(): lax.dot_general(window, filt_local[slot_index, row_tap, col_tap], (((3,),...  16.8 us
    dot_general x36, matrix products, filter_terms(): lax.dot_general(window, gradient, (((0, 1, 2), (0, 1, 2)), ((), ())), pre...  14.7 us
    all_gather x1, blocking collectives, shards(): all_grad_one = lax.all_gather(grad_one_rim, 'rot', axis=0, tiled=True)  10.2 us
    all_gather x1, blocking collectives, shards(): lax.all_gather(grad_rim, 'rot', axis=0, tiled=True)  9.99 us
    all_gather x1, blocking collectives, shards(): lax.all_gather(inputs_rim, 'rot', axis=0, tiled=True)  9.96 us
    all_gather x1, blocking collectives, shards(): lax.all_gather(act_rim, 'rot', axis=0, tiled=True)  9.19 us
  transfers between devices with their start and end apart: 7, of which 7 were waited for; matrix products, arithmetic and copies ran while one was open for 10% of the time, Pallas kernels for 0%

commit v1 on v0

--- a/solution.py
+++ b/solution.py
@@ -2,6 +2,12 @@
 import jax.numpy as jnp
 from jax import lax
 from jax.sharding import PartitionSpec as P
+
+
+def add_all(x, axis):
+    parts = lax.all_gather(x, axis, axis=0, tiled=False)
+    total = parts.sum(axis=0)
+    return total
 
 
 def with_halo(block, sides, width):
@@ -142,7 +148,7 @@
     )
     filt_part_one = filter_terms(all_inputs, all_grad_one[:, :, 1:-1], my_rank, per_dev)
     summed_one, summed_two = (
-        lax.psum(filt_part_one.astype(jnp.bfloat16), "az").astype(jnp.float32),
+        add_all(filt_part_one.astype(jnp.bfloat16), "az").astype(jnp.float32),
         lax.psum(filt_part_two.astype(jnp.bfloat16), "az").astype(jnp.float32),
     )
     return (input_sum, summed_one * norm_scale, summed_two * norm_scale)

time: 205 us -> 181 us (0.88)
  waiting for transfers between devices: 94.8 us -> 66.2 us
  other arithmetic: 13 us -> 15.4 us
    all_gather x0 -> x1, waiting for transfers between devices: none -> 49.1 us  [add_all(): parts = lax.all_gather(x, axis, axis=0, tiled=False)]
    psum x1, waiting for transfers between devices: 47.2 us -> 3.56 us  [shards(): lax.psum(filt_part_two.astype(jnp.bfloat16), 'az').astype(jnp.float32)]
    reduce_scatter x1, waiting for transfers between devices: 33.8 us -> 0.01 us  [shards(): lax.psum_scatter(make_terms(doubled_one, my_rank, filt_one, row_count, co...]
    reduce_sum x0 -> x1, other arithmetic: none -> 2.15 us  [add_all(): total = parts.sum(axis=0)]
  transfers between devices with their start and end apart: 7 -> 8, of which waited for: 7 -> 7; matrix products, arithmetic and copies ran while one was open for 10% -> 21% of each run, Pallas kernels for 0% -> 0%
where the time goes in v1:
time: 181 us; the launch traced here: 180 us
  waiting for transfers between devices  66.2 us (37%)
  blocking collectives  39.3 us (22%)
  matrix products  32.3 us (18%)
  between operations  15.9 us (9%)
  other arithmetic  15.4 us (9%)
  starting transfers between devices  8.95 us (5%)
  local copies, waits for them, and re-layouts  1.93 us (1%)
    all_gather x1, waiting for transfers between devices, add_all(): parts = lax.all_gather(x, axis, axis=0, tiled=False)  49.1 us
    dot_general x36, matrix products, make_terms(): lax.dot_general(window, filt_local[slot_index, row_tap, col_tap], (((3,),...  17.7 us
    dot_general x36, matrix products, filter_terms(): lax.dot_general(window, gradient, (((0, 1, 2), (0, 1, 2)), ((), ())), pre...  14.7 us
    all_gather x1, blocking collectives, shards(): all_grad_one = lax.all_gather(grad_one_rim, 'rot', axis=0, tiled=True)  10.2 us
    all_gather x1, blocking collectives, shards(): lax.all_gather(grad_rim, 'rot', axis=0, tiled=True)  9.99 us
    all_gather x1, blocking collectives, shards(): lax.all_gather(inputs_rim, 'rot', axis=0, tiled=True)  9.96 us
    all_gather x1, blocking collectives, shards(): lax.all_gather(act_rim, 'rot', axis=0, tiled=True)  9.18 us
    ppermute x2, starting transfers between devices, with_halo(): lax.ppermute(lax.slice_in_dim(block, 0, width, axis=dim), axis, backward)  8.51 us
  transfers between devices with their start and end apart: 8, of which 7 were waited for; matrix products, arithmetic and copies ran while one was open for 21% of the time, Pallas kernels for 0%

profile of v1, /device:TPU:0, one launch (start us, length us, event | category | flops | bytes accessed | tf_op | source)
XLA Modules:
  0.0 180.0 jit_solution(15355442952701883251)
XLA Ops:
  9.8 5.1 %collective-permute-start.1 = (bf16[6,4,1,128]{3,2,1,0:T(2,128)(2,1)S(1)}, bf16[6,4,1,128]{3,2,1,0:T(2,128)(2,1)S(1)}, u32[]{:S(2)}, u32[]{:S(2)}) collective-permute-start(bf16[6,4,1,128]{3,2,1,0:T(2,128)(2,1)S(1)} %get-tuple-element.15), channel_id=1, source_target_pairs={{1,0},{2,1},{3,2},{0,3},{5,4},{6,5},{7,6},{4,7},{9,8},{10,9},{11,1... | collective-permute-start | bytes 18440 | tf_op jit(solution)/shard_map/ppermute | solution.py:22
  14.9 1.4 collective-permute-done.1
  16.3 4.1 %collective-permute-done = bf16[6,4,1,128]{3,2,1,0:T(2,128)(2,1)S(1)} collective-permute-done((bf16[6,4,1,128]{3,2,1,0:T(2,128)(2,1)S(1)}, bf16[6,4,1,128]{3,2,1,0:T(2,128)(2,1)S(1)}, u32[]{:S(2)}, u32[]{:S(2)}) %collective-permute-start) | collective-permute-done | bytes 6176 | tf_op jit(solution)/shard_map/ppermute | solution.py:19
  21.5 10.0 %all_gather.16 = bf16[16,4,34,128]{3,1,2,0:T(4,128)(2,1)S(1)} all-gather(bf16[2,4,34,128]{3,1,2,0:T(4,128)(2,1)S(1)} %copy.9), channel_id=1, replica_groups=mesh['rot'=8,'az'=4] {'rot'}, dimensions={0}, use_global_device_ids=true | all-gather | bytes 626688 | tf_op jit(solution)/shard_map/all_gather | solution.py:110
  38.0 1.3 convolution_add_fusion.17
  39.4 10.0 %all_gather.18 = bf16[16,4,34,128]{3,1,2,0:T(4,128)(2,1)S(1)} all-gather(bf16[2,4,34,128]{3,1,2,0:T(4,128)(2,1)S(1)} %copy.13), channel_id=1, replica_groups=mesh['rot'=8,'az'=4] {'rot'}, dimensions={0}, use_global_device_ids=true | all-gather | bytes 626688 | tf_op jit(solution)/shard_map/all_gather | solution.py:108
  49.6 9.2 %all_gather.20 = bf16[16,4,34,128]{3,1,2,0:T(4,128)(2,1)S(1)} all-gather(bf16[2,4,34,128]{3,1,2,0:T(4,128)(2,1)S(1)} %copy.16), channel_id=1, replica_groups=mesh['rot'=8,'az'=4] {'rot'}, dimensions={0}, use_global_device_ids=true | all-gather | bytes 626688 | tf_op jit(solution)/shard_map/all_gather | solution.py:109
  64.7 2.1 %fusion.112 = (bf16[16,6,34,128]{3,2,1,0:T(8,128)(2,1)}, bf16[16,6,34,128]{3,2,1,0:T(8,128)(2,1)}) fusion(s32[]{:T(128)S(6)} %select_n.35, bf16[16,6,34,128]{3,2,1,0:T(8,128)(2,1)S(1)} %pad.15, s32[]{:T(128)S(6)} %select_n.36), kind=kLoop, calls=%fused_computation.200 | loop fusion | flops 835584 | bytes 2506760 | tf_op jit(solution)/shard_map/concatenate | solution.py:39
  69.2 3.5 %reduce-scatter.3.cloned.1.call-done = f32[2,4,32,128]{3,2,1,0:T(8,128)} async-done(((f32[16,4,32,128]{3,2,1,0:T(8,128)}), f32[2,4,32,128]{3,2,1,0:T(8,128)}) %reduce-scatter.3.cloned.1.call-update) | async-done | bytes 131088 | tf_op jit(solution)/shard_map/reduce_scatter | solution.py:115
  73.7 3.4 %collective-permute-start.3 = (bf16[2,4,1,128]{3,2,1,0:T(2,128)(2,1)S(1)}, bf16[2,4,1,128]{3,2,1,0:T(2,128)(2,1)S(1)}, u32[]{:S(2)}, u32[]{:S(2)}) collective-permute-start(bf16[2,4,1,128]{3,2,1,0:T(2,128)(2,1)S(1)} %get-tuple-element.17), channel_id=1, source_target_pairs={{1,0},{2,1},{3,2},{0,3},{5,4},{6,5},{7,6},{4,7},{9,8},{10,9},{11,1... | collective-permute-start | bytes 6152 | tf_op jit(solution)/shard_map/ppermute | solution.py:22
  78.4 4.1 %collective-permute-done.2 = bf16[2,4,1,128]{3,2,1,0:T(2,128)(2,1)S(1)} collective-permute-done((bf16[2,4,1,128]{3,2,1,0:T(2,128)(2,1)S(1)}, bf16[2,4,1,128]{3,2,1,0:T(2,128)(2,1)S(1)}, u32[]{:S(2)}, u32[]{:S(2)}) %collective-permute-start.2) | collective-permute-done | bytes 2080 | tf_op jit(solution)/shard_map/ppermute | solution.py:19
  82.6 10.2 %all_gather.17 = bf16[16,4,34,128]{3,1,2,0:T(4,128)(2,1)S(1)} all-gather(bf16[2,4,34,128]{3,1,2,0:T(4,128)(2,1)S(1)} %copy.11), channel_id=1, replica_groups=mesh['rot'=8,'az'=4] {'rot'}, dimensions={0}, use_global_device_ids=true | all-gather | bytes 626688 | tf_op jit(solution)/shard_map/all_gather | solution.py:133
  93.7 1.1 fusion.170
  94.8 1.1 convolution_add_fusion.16
  95.9 1.1 convolution_add_fusion.15
  106.1 1.1 convolution_add_fusion.14
  107.2 1.1 convolution_add_fusion.13
  108.6 1.1 convolution_add_fusion.12
  113.2 1.1 fusion
  114.4 3.6 %all-reduce.6.cloned.1.call-done = bf16[2,3,3,128,128]{4,3,2,1,0:T(8,128)(2,1)} async-done(((bf16[2,3,3,128,128]{4,3,2,1,0:T(8,128)(2,1)}), bf16[2,3,3,128,128]{4,3,2,1,0:T(8,128)(2,1)}) %all-reduce.6.cloned.1.call-update) | async-done | bytes 589840 | tf_op jit(solution)/shard_map/psum | solution.py:152
  117.9 2.2 %convert_multiply_fusion = f32[2,3,3,128,128]{4,3,2,1,0:T(8,128)} fusion(bf16[2,3,3,128,128]{4,3,2,1,0:T(8,128)(2,1)} %all-reduce.6.cloned.1.call-done), kind=kLoop, calls=%fused_computation.51 | loop fusion | flops 589824 | bytes 1769472 | tf_op jit(solution)/shard_map/mul | solution.py:154
  120.1 49.1 %all-gather.2.cloned.1.call-done = bf16[4,2,3,3,128,128]{5,4,3,2,1,0:T(8,128)(2,1)} async-done(((bf16[1,2,3,3,128,128]{5,4,3,2,1,0:T(8,128)(2,1)}), bf16[4,2,3,3,128,128]{5,4,3,2,1,0:T(8,128)(2,1)}) %all-gather.2.cloned.1.call-update) | async-done | bytes 2359312 | tf_op jit(solution)/shard_map/all_gather | solution.py:8
  169.3 2.2 %reduce_sum.12 = bf16[2,3,3,128,128]{4,3,2,1,0:T(8,128)(2,1)S(1)} reduce(bf16[4,2,3,3,128,128]{5,4,3,2,1,0:T(8,128)(2,1)} %all-gather.2.cloned.1.call-done, bf16[]{:T(256)} %constant.35.clone.1), dimensions={0}, to_apply=%region_2.3 | reduce | flops 884736 | bytes 2949122 | tf_op jit(solution)/shard_map/reduce_sum | solution.py:9
  171.4 1.2 convert_multiply_fusion.1
  (110 shorter events, 34.0 us)
Async XLA Ops:
  8.0 64.7 %reduce-scatter.3.cloned.1.call-start = ((), (), s32[]{:S(2)}) async-start(), calls=%async_computation.2 | async-start | bytes 1179648 | tf_op jit(solution)/shard_map/reduce_scatter | solution.py:115
  9.8 6.5 %collective-permute-start.1 = (bf16[6,4,1,128]{3,2,1,0:T(2,128)(2,1)S(1)}, bf16[6,4,1,128]{3,2,1,0:T(2,128)(2,1)S(1)}, u32[]{:S(2)}, u32[]{:S(2)}) collective-permute-start(bf16[6,4,1,128]{3,2,1,0:T(2,128)(2,1)S(1)} %get-tuple-element.15), channel_id=1, source_target_pairs={{1,0},{2,1},{3,2},{0,3},{5,4},{6,5},{7,6},{4,7},{9,8},{10,9},{11,1... | collective-permute-start | bytes 18440 | tf_op jit(solution)/shard_map/ppermute | solution.py:22
  14.9 5.5 %collective-permute-start = (bf16[6,4,1,128]{3,2,1,0:T(2,128)(2,1)S(1)}, bf16[6,4,1,128]{3,2,1,0:T(2,128)(2,1)S(1)}, u32[]{:S(2)}, u32[]{:S(2)}) collective-permute-start(bf16[6,4,1,128]{3,2,1,0:T(2,128)(2,1)S(1)} %get-tuple-element.14), channel_id=1, source_target_pairs={{0,1},{1,2},{2,3},{3,0},{4,5},{5,6},{6,7},{7,4},{8,9},{9,10},{10,1... | collective-permute-start | bytes 18440 | tf_op jit(solution)/shard_map/ppermute | solution.py:19
  31.6 1.1 copy-start.3
  39.3 78.6 %all-reduce.6.cloned.1.call-start = ((), (), s32[]{:S(2)}) async-start(), calls=%async_computation.5 | async-start | bytes 1179648 | tf_op jit(solution)/shard_map/psum | solution.py:152
  68.8 3.9 %copy-start.4 = (bf16[2,4,32,128]{3,2,1,0:T(8,128)(2,1)S(1)}, bf16[2,4,32,128]{3,2,1,0:T(8,128)(2,1)}, u32[]{:S(2)}) copy-start(bf16[2,4,32,128]{3,2,1,0:T(8,128)(2,1)} %param.7) | copy-start | bytes 196612
  73.7 4.7 %collective-permute-start.3 = (bf16[2,4,1,128]{3,2,1,0:T(2,128)(2,1)S(1)}, bf16[2,4,1,128]{3,2,1,0:T(2,128)(2,1)S(1)}, u32[]{:S(2)}, u32[]{:S(2)}) collective-permute-start(bf16[2,4,1,128]{3,2,1,0:T(2,128)(2,1)S(1)} %get-tuple-element.17), channel_id=1, source_target_pairs={{1,0},{2,1},{3,2},{0,3},{5,4},{6,5},{7,6},{4,7},{9,8},{10,9},{11,1... | collective-permute-start | bytes 6152 | tf_op jit(solution)/shard_map/ppermute | solution.py:22
  77.1 5.4 %collective-permute-start.2 = (bf16[2,4,1,128]{3,2,1,0:T(2,128)(2,1)S(1)}, bf16[2,4,1,128]{3,2,1,0:T(2,128)(2,1)S(1)}, u32[]{:S(2)}, u32[]{:S(2)}) collective-permute-start(bf16[2,4,1,128]{3,2,1,0:T(2,128)(2,1)S(1)} %get-tuple-element.16), channel_id=1, source_target_pairs={{0,1},{1,2},{2,3},{3,0},{4,5},{5,6},{6,7},{7,4},{8,9},{9,10},{10,1... | collective-permute-start | bytes 6152 | tf_op jit(solution)/shard_map/ppermute | solution.py:19
  78.0 91.3 %all-gather.2.cloned.1.call-start = ((), (), s32[]{:S(2)}) async-start(), calls=%async_computation.4 | async-start | bytes 2949120 | tf_op jit(solution)/shard_map/all_gather | solution.py:8
  95.9 1.2 copy-start.1
  100.4 1.2 copy-start
  108.3 64.3 %reduce-scatter.5.cloned.1.call-start = ((), (), s32[]{:S(2)}) async-start(), calls=%async_computation.3 | async-start | bytes 589824 | tf_op jit(solution)/shard_map/reduce_scatter | solution.py:135
  108.6 1.1 copy-start.2
Sparse Core Ops, SparseCore 0:
  39.4 33.2 reduce-scatter.2
  114.5 31.3 reduce-scatter.4
Sparse Core Ops, SparseCore 1:
  78.1 39.8 all-reduce.5
  119.9 49.3 all-gather.1
